TPU v7x, 256 devices: a whole 4x4x8 slice. The times are simulated.
256 devices in a mesh: section: 2 (over core), seq: 16 (over y, x), mp: 8 (over z).
Axes of the slice: x: 4, y: 4, z: 8, core: 2. Of those that a mesh axis runs over, the one named last changes fastest.
Arguments:
- stream: bfloat16 [2, 2048, 3584], P(None, 'seq', 'mp'), may hold values from -6 to 6
- segment_ids: int32 [2, 2048], P(None, 'seq'), may hold values from 0 to 1, never falling along the last dimension, each value on 1 to 1536 neighbouring positions
- norm_gain: bfloat16 [2, 3584], P('section'), may hold values from 0.5 to 1.5
- in_weight: bfloat16 [2, 3584, 2, 4096], P('section', None, None, 'mp'), may hold values from -0.09375 to 0.09375
- bc_weight: bfloat16 [2, 3584, 128], P('section'), may hold values from -0.09375 to 0.09375
- dt_weight: bfloat16 [2, 3584, 64], P('section', None, 'mp'), may hold values from -0.09375 to 0.09375
- dt_bias: float32 [2, 64], P('section', 'mp'), may hold values from -4 to -1
- decay_rate: float32 [2, 64], P('section', 'mp'), may hold values from 0.001 to 0.5
- conv_inner: float32 [2, 4, 4096], P('section', None, 'mp'), may hold values from -3 to 3
- conv_state: float32 [2, 4, 128], P('section'), may hold values from -3 to 3
- skip_gain: float32 [2, 64], P('section', 'mp'), may hold values from 0.5 to 1.5
- inner_gain: bfloat16 [2, 4096], P('section', 'mp'), may hold values from 0.5 to 1.5
- out_weight: bfloat16 [2, 4096, 3584], P('section', 'mp'), may hold values from -0.09375 to 0.09375
Outputs:
- hidden: bfloat16 [2, 2, 2048, 3584], P('section', None, 'seq', 'mp')
Inputs may be any that keep to these rules, and one draw needn't show every extreme that they name: `segment_ids`: within each micro-batch the document numbers start at 0 and rise by one at each new document; a document has 1 to 1536 positions.
All inputs are finite; a program needn't handle non-finite values.
Results may differ from a plain program's by a relative error of at most 0.023.
Values may be sent and summed in bfloat16 or wider, within the bound.
A program may use at most 128 MiB of HBM per device.

v0:
```python
import jax
import jax.numpy as jnp
from jax import lax
from jax.sharding import PartitionSpec as P

HDIM = 64
STATE = 64
INNER = 4096
EPS = 1e-05


def shifted(block, axis, distance):
    devices = range(lax.axis_size(axis))
    route = [(i - distance, i) for i in devices if i - distance in devices]
    return lax.ppermute(block, axis, route)


def norm_rows(hidden_rows, gain):
    values = hidden_rows.astype(jnp.float32)
    scale = lax.rsqrt(jnp.mean(values * values, axis=-1, keepdims=True) + EPS)
    return (values * scale * gain.astype(jnp.float32)).astype(jnp.bfloat16)


def causal_conv(padded, pad_docs, documents, taps):
    length = documents.shape[0]
    total = jnp.zeros((length, padded.shape[1]), jnp.float32)
    for offset in range(taps.shape[0]):
        match = (pad_docs[offset : offset + length] == documents)[:, None]
        term = padded[offset : offset + length].astype(jnp.float32) * taps[offset][None, :]
        total = total + jnp.where(match, term, 0.0)
    return jax.nn.silu(total).astype(jnp.bfloat16)


def block_terms(inputs, b_rows, c_rows, steps_dt, documents, prior_doc, decay_rate):
    length = documents.shape[0]
    cumlog = jnp.cumsum(-steps_dt * decay_rate[None, :], axis=0)
    places = jnp.arange(length, dtype=jnp.int32)
    same_doc = (documents[:, None] == documents[None, :]) & (places[:, None] >= places[None, :])
    gap_log = jnp.where(same_doc[:, :, None], cumlog[:, None, :] - cumlog[None, :, :], 0.0)
    decays = jnp.where(same_doc[:, :, None], jnp.exp(gap_log), 0.0)
    intersection = jnp.dot(c_rows, b_rows.T, preferred_element_type=jnp.float32)
    mixing = (decays * intersection[:, :, None] * steps_dt[None, :, :]).astype(jnp.bfloat16)
    local_out = jnp.einsum("tsh,shp->thp", mixing, inputs, preferred_element_type=jnp.float32)
    carry_in = jnp.where((documents == prior_doc)[:, None], jnp.exp(cumlog), 0.0)
    last_doc = documents[-1]
    tail_weight = (
        jnp.where((documents == last_doc)[:, None], jnp.exp(cumlog[-1][None, :] - cumlog), 0.0)
        * steps_dt
    )
    local_state = jnp.einsum(
        "sh,shp,sn->hpn",
        tail_weight,
        inputs.astype(jnp.float32),
        b_rows.astype(jnp.float32),
        precision=lax.Precision.HIGHEST,
    )
    through = jnp.where(last_doc == prior_doc, jnp.exp(cumlog[-1]), 0.0)
    return (local_out, carry_in, local_state, through)


def mixer_layer(
    hidden_rows,
    documents,
    norm_gain,
    in_weight,
    bc_weight,
    dt_weight,
    dt_bias,
    decay_rate,
    conv_inner,
    conv_state,
    skip_gain,
    inner_gain,
    out_weight,
):
    whole = lax.all_gather(hidden_rows, "mp", axis=1, tiled=True)
    normed = norm_rows(whole, norm_gain)
    width_loc = in_weight.shape[-1]
    both = jnp.dot(
        normed, in_weight.reshape(in_weight.shape[0], -1), preferred_element_type=jnp.float32
    )
    inner_raw = both[:, :width_loc]
    gate_raw = both[:, width_loc:]
    state_raw = jnp.dot(normed, bc_weight, preferred_element_type=jnp.float32)
    dt_raw = jnp.dot(normed, dt_weight, preferred_element_type=jnp.float32)
    joined = jnp.concatenate([inner_raw, state_raw], axis=1).astype(jnp.bfloat16)
    taps = jnp.concatenate([conv_inner, conv_state], axis=1)
    lag = taps.shape[0] - 1
    rim_rows, rim_docs = shifted((joined[-lag:], documents[-lag:]), "seq", 1)
    padded = jnp.concatenate([rim_rows, joined], axis=0)
    pad_docs = jnp.concatenate([rim_docs, documents], axis=0)
    mixed_in = causal_conv(padded, pad_docs, documents, taps)
    length = documents.shape[0]
    heads = width_loc // HDIM
    inputs = mixed_in[:, :width_loc].reshape(length, heads, HDIM)
    b_rows = mixed_in[:, width_loc : width_loc + STATE]
    c_rows = mixed_in[:, width_loc + STATE :]
    steps_dt = jax.nn.softplus(dt_raw + dt_bias[None, :])
    local_out, carry_in, local_state, through = block_terms(
        inputs, b_rows, c_rows, steps_dt, documents, rim_docs[-1], decay_rate
    )

    def relay(turn_index, state_in):
        return shifted(
            (through[:, None, None] * state_in + local_state).astype(jnp.bfloat16), "seq", 1
        ).astype(jnp.float32)

    state_in = lax.fori_loop(0, lax.axis_size("seq") - 1, relay, jnp.zeros_like(local_state))
    from_state = jnp.einsum(
        "tn,hpn->thp", c_rows.astype(jnp.float32), state_in, precision=lax.Precision.HIGHEST
    )
    results = (
        local_out
        + carry_in[:, :, None] * from_state
        + skip_gain[None, :, None] * inputs.astype(jnp.float32)
    )
    gated = results.reshape(length, width_loc) * jax.nn.silu(gate_raw)
    squares = lax.psum(jnp.sum(gated * gated, axis=-1), "mp")
    scale = lax.rsqrt(squares / INNER + EPS)
    normed_inner = (gated * scale[:, None] * inner_gain.astype(jnp.float32)).astype(jnp.bfloat16)
    update = jnp.dot(normed_inner, out_weight, preferred_element_type=jnp.float32)
    summed = lax.psum_scatter(
        update.astype(jnp.bfloat16), "mp", scatter_dimension=1, tiled=True
    ).astype(jnp.float32)
    return (hidden_rows.astype(jnp.float32) + summed).astype(jnp.bfloat16)


def per_device(
    stream,
    segment_ids,
    norm_gain,
    in_weight,
    bc_weight,
    dt_weight,
    dt_bias,
    decay_rate,
    conv_inner,
    conv_state,
    skip_gain,
    inner_gain,
    out_weight,
):
    first = lax.axis_index("section") == 0
    count = stream.shape[0]
    out_layer = out_weight[0]
    received = jnp.zeros_like(stream[0])
    outputs = []
    for step_index in range(count + 1):
        own_rows = stream[min(step_index, count - 1)]
        own_docs = jnp.where(
            first, segment_ids[min(step_index, count - 1)], segment_ids[max(step_index - 1, 0)]
        )
        layer_in = jnp.where(first, own_rows, received)
        result = mixer_layer(
            layer_in,
            own_docs,
            norm_gain[0],
            in_weight[0],
            bc_weight[0],
            dt_weight[0],
            dt_bias[0],
            decay_rate[0],
            conv_inner[0],
            conv_state[0],
            skip_gain[0],
            inner_gain[0],
            out_layer,
        )
        outputs.append(result)
        if step_index < count:
            received = shifted(result, "section", 1)
    final = jnp.stack(
        [
            jnp.where(first, outputs[index_micro], outputs[index_micro + 1])
            for index_micro in range(count)
        ]
    )
    return final[None]


def solution(mesh):
    placed = (
        P(None, "seq", "mp"),
        P(None, "seq"),
        P("section", None),
        P("section", None, None, "mp"),
        P("section", None, None),
        P("section", None, "mp"),
        P("section", "mp"),
        P("section", "mp"),
        P("section", None, "mp"),
        P("section", None, None),
        P("section", "mp"),
        P("section", "mp"),
        P("section", "mp", None),
    )
    return jax.shard_map(
        per_device,
        mesh=mesh,
        in_specs=placed,
        out_specs=P("section", None, "seq", "mp"),
        check_vma=False,
    )
```

profile of v0, /device:TPU:2, one launch (start us, length us, event | category | flops | bytes accessed | tf_op | source)
XLA Modules:
  0.0 758.4 jit_solution(8213100159065672628)
XLA Ops:
  7.5 30.2 %all-gather = bf16[1,128,3584]{1,2,0:T(8,128)(2,1)S(1)} all-gather(bf16[1,128,448]{1,2,0:T(8,128)(2,1)S(1)} %slice_select_fusion), channel_id=2, replica_groups=mesh['section'=2,'seq'=16,'mp'=8] {'mp'}, dimensions={2}, use_global_device_ids=true | all-gather | bytes 1032192 | tf_op jit(solution)/shard_map/all_gather | solution.py:76
  38.3 5.4 copy.80
  66.2 130.9 %while.33 = (s32[]{:T(128)}, f32[8,64,64]{2,1,0:T(8,128)S(1)}, f32[8]{0:T(128)S(1)}, f32[8,64,64]{2,1,0:T(8,128)S(1)}, s32[]{:T(128)}, /*index=5*/s32[]{:T(128)}) while((s32[]{:T(128)}, f32[8,64,64]{2,1,0:T(8,128)S(1)}, f32[8]{0:T(128)S(1)}, f32[8,64,64]{2,1,0:T(8,128)S(1)}, s32[]{:T(128)}, /*index=5*/s32[]{:T(128)}) %tuple.86), condition=%wide.region_3.4_spmd.clone, body=%wide.region_2.3_spmd.clone.sunk | while | flops 163843 | bytes 786583 | solution.py:108
  87.3 5.2 collective-permute-start
  95.2 6.5 collective-permute-start
  104.4 6.5 collective-permute-start
  113.5 6.5 collective-permute-start
  122.6 6.5 collective-permute-start
  132.0 6.8 collective-permute-start
  138.7 3.8 collective-permute-done
  142.7 6.4 collective-permute-start
  152.0 6.0 collective-permute-start
  160.7 6.5 collective-permute-start
  169.8 6.5 collective-permute-start
  178.9 6.5 collective-permute-start
  188.1 6.5 collective-permute-start
  197.7 16.1 %psum.21 = f32[128]{0:T(128)S(1)} all-reduce(f32[128]{0:T(128)S(1)} %multiply_reduce_fusion.2), channel_id=1, replica_groups=mesh['section'=2,'seq'=16,'mp'=8] {'mp'}, use_global_device_ids=true, to_apply=%region_5.6 | all-reduce | flops 128 | bytes 1024 | tf_op jit(solution)/shard_map/psum | solution.py:118
  213.9 4.6 convolution_convert_fusion.2
  218.6 6.4 collective-permute-start.6
  228.2 34.4 %reduce-scatter.4.cloned.1.call-done = bf16[128,448]{0,1:T(8,128)(2,1)} async-done(((bf16[128,3584]{0,1:T(8,128)(2,1)}), bf16[128,448]{0,1:T(8,128)(2,1)}) %reduce-scatter.4.cloned.1.call-update) | async-done | bytes 114704 | tf_op jit(solution)/shard_map/reduce_scatter | solution.py:122
  266.1 26.7 %all_gather.10 = bf16[128,3584]{0,1:T(8,128)(2,1)S(1)} all-gather(bf16[128,448]{0,1:T(8,128)(2,1)S(1)} %bitcast_select_fusion.1), channel_id=1, replica_groups=mesh['section'=2,'seq'=16,'mp'=8] {'mp'}, dimensions={1}, use_global_device_ids=true | all-gather | bytes 1032192 | tf_op jit(solution)/shard_map/all_gather | solution.py:76
  294.4 5.1 fusion.117
  307.4 132.7 %while.34 = (s32[]{:T(128)}, f32[8,64,64]{2,1,0:T(8,128)S(1)}, f32[8]{0:T(128)S(1)}, f32[8,64,64]{2,1,0:T(8,128)S(1)}, s32[]{:T(128)}, /*index=5*/s32[]{:T(128)}) while((s32[]{:T(128)}, f32[8,64,64]{2,1,0:T(8,128)S(1)}, f32[8]{0:T(128)S(1)}, f32[8,64,64]{2,1,0:T(8,128)S(1)}, s32[]{:T(128)}, /*index=5*/s32[]{:T(128)}) %tuple.89), condition=%wide.region_10.11_spmd.clone, body=%wide.region_9.10_spmd.clone.sunk | while | flops 163843 | bytes 786583 | solution.py:108
  310.9 3.5 collective-permute-done.1
  317.9 3.5 collective-permute-done.1
  321.5 5.1 collective-permute-start.1
  329.3 6.3 collective-permute-start.1
  338.2 6.5 collective-permute-start.1
  347.4 6.5 collective-permute-start.1
  356.5 6.5 collective-permute-start.1
  365.6 6.5 collective-permute-start.1
  375.0 6.8 collective-permute-start.1
  381.8 3.8 collective-permute-done.1
  385.7 6.4 collective-permute-start.1
  395.0 6.0 collective-permute-start.1
  403.7 6.5 collective-permute-start.1
  412.9 6.5 collective-permute-start.1
  422.0 6.5 collective-permute-start.1
  431.1 6.5 collective-permute-start.1
  440.8 15.9 %psum.22 = f32[128]{0:T(128)S(1)} all-reduce(f32[128]{0:T(128)S(1)} %multiply_reduce_fusion.1), channel_id=1, replica_groups=mesh['section'=2,'seq'=16,'mp'=8] {'mp'}, use_global_device_ids=true, to_apply=%region_12.13 | all-reduce | flops 128 | bytes 1024 | tf_op jit(solution)/shard_map/psum | solution.py:118
  456.7 4.5 convolution_convert_fusion.1
  461.3 45.0 %reduce-scatter.6.cloned.1.call-done = bf16[128,448]{0,1:T(8,128)(2,1)} async-done(((bf16[128,3584]{0,1:T(8,128)(2,1)}), bf16[128,448]{0,1:T(8,128)(2,1)}) %reduce-scatter.6.cloned.1.call-update) | async-done | bytes 114704 | tf_op jit(solution)/shard_map/reduce_scatter | solution.py:122
  510.0 26.5 %all_gather.11 = bf16[128,3584]{0,1:T(8,128)(2,1)S(1)} all-gather(bf16[128,448]{0,1:T(8,128)(2,1)S(1)} %bitcast_select_fusion), channel_id=1, replica_groups=mesh['section'=2,'seq'=16,'mp'=8] {'mp'}, dimensions={1}, use_global_device_ids=true | all-gather | bytes 1032192 | tf_op jit(solution)/shard_map/all_gather | solution.py:76
  538.0 5.1 fusion.113
  551.0 132.5 %while.35 = (s32[]{:T(128)}, f32[8,64,64]{2,1,0:T(8,128)S(1)}, f32[8]{0:T(128)S(1)}, f32[8,64,64]{2,1,0:T(8,128)S(1)}, s32[]{:T(128)}, /*index=5*/s32[]{:T(128)}) while((s32[]{:T(128)}, f32[8,64,64]{2,1,0:T(8,128)S(1)}, f32[8]{0:T(128)S(1)}, f32[8,64,64]{2,1,0:T(8,128)S(1)}, s32[]{:T(128)}, /*index=5*/s32[]{:T(128)}) %tuple.92), condition=%wide.region_17.18_spmd.clone, body=%wide.region_16.17_spmd.clone.sunk | while | flops 163843 | bytes 786583 | solution.py:108
  554.5 3.5 collective-permute-done.2
  561.6 3.5 collective-permute-done.2
  565.2 4.7 collective-permute-start.2
  572.6 6.5 collective-permute-start.2
  581.7 6.5 collective-permute-start.2
  590.9 6.5 collective-permute-start.2
  600.0 6.5 collective-permute-start.2
  609.1 6.5 collective-permute-start.2
  618.6 6.8 collective-permute-start.2
  625.4 3.6 collective-permute-done.2
  629.2 6.5 collective-permute-start.2
  638.3 6.2 collective-permute-start.2
  647.2 6.5 collective-permute-start.2
  656.3 6.5 collective-permute-start.2
  665.4 6.5 collective-permute-start.2
  674.6 6.5 collective-permute-start.2
  684.2 16.1 %psum.23 = f32[128]{0:T(128)S(1)} all-reduce(f32[128]{0:T(128)S(1)} %multiply_reduce_fusion), channel_id=1, replica_groups=mesh['section'=2,'seq'=16,'mp'=8] {'mp'}, use_global_device_ids=true, to_apply=%region_19.20 | all-reduce | flops 128 | bytes 1024 | tf_op jit(solution)/shard_map/psum | solution.py:118
  700.3 4.5 convolution_convert_fusion
  704.9 45.3 %reduce-scatter.8.cloned.1.call-done = bf16[128,448]{0,1:T(8,128)(2,1)} async-done(((bf16[128,3584]{0,1:T(8,128)(2,1)}), bf16[128,448]{0,1:T(8,128)(2,1)}) %reduce-scatter.8.cloned.1.call-update) | async-done | bytes 114704 | tf_op jit(solution)/shard_map/reduce_scatter | solution.py:122
  (283 shorter events, 181.1 us)
Async XLA Ops:
  6.5 40.2 %copy-start = (bf16[1,3584,128]{2,1,0:T(8,128)(2,1)S(1)}, bf16[1,3584,128]{2,1,0:T(8,128)(2,1)}, u32[]{:S(2)}) copy-start(bf16[1,3584,128]{2,1,0:T(8,128)(2,1)} %param.23) | copy-start | bytes 2752516
  6.5 31.7 %copy-start.4 = (bf16[1,3584]{1,0:T(2,128)(2,1)S(1)}, bf16[1,3584]{1,0:T(2,128)(2,1)}, u32[]{:S(2)}) copy-start(bf16[1,3584]{1,0:T(2,128)(2,1)} %param.21) | copy-start | bytes 21508
  6.5 256.1 %reduce-scatter.4.cloned.1.call-start = ((), (), s32[]{:S(2)}) async-start(), calls=%async_computation.3 | async-start | bytes 1032192 | tf_op jit(solution)/shard_map/reduce_scatter | solution.py:122
  46.7 13.5 %copy-start.7 = (bf16[1,512]{1,0:T(2,128)(2,1)S(1)}, bf16[1,512]{1,0:T(2,128)(2,1)}, u32[]{:S(2)}) copy-start(bf16[1,512]{1,0:T(2,128)(2,1)} %param.30) | copy-start | bytes 3076
  46.7 13.5 %copy-start.5 = (f32[1,4,512]{2,1,0:T(4,128)S(1)}, f32[1,4,512]{2,1,0:T(4,128)}, u32[]{:S(2)}) copy-start(f32[1,4,512]{2,1,0:T(4,128)} %param.27) | copy-start | bytes 24580
  46.7 13.5 %copy-start.8 = (f32[1,4,128]{2,1,0:T(4,128)S(1)}, f32[1,4,128]{2,1,0:T(4,128)}, u32[]{:S(2)}) copy-start(f32[1,4,128]{2,1,0:T(4,128)} %param.28) | copy-start | bytes 6148
  47.7 17.1 %collective-permute-start.4 = (bf16[3,640]{1,0:T(4,128)(2,1)S(1)}, bf16[3,640]{1,0:T(4,128)(2,1)S(1)}, u32[]{:S(2)}, u32[]{:S(2)}) collective-permute-start(bf16[3,640]{1,0:T(4,128)(2,1)S(1)} %fusion.89), channel_id=1, source_target_pairs={{0,8},{8,16},{16,24},{24,32},{32,40},{40,48},{48,56},{56,64},{64,7... | collective-permute-start | bytes 11528 | tf_op jit(solution)/shard_map/ppermute | solution.py:15
  51.2 9.0 %collective-permute-start.3 = (s32[3]{0:T(128)S(1)}, s32[3]{0:T(128)S(1)}, u32[]{:S(2)}, u32[]{:S(2)}) collective-permute-start(s32[3]{0:T(128)S(1)} %get-tuple-element.173), channel_id=1, source_target_pairs={{0,8},{8,16},{16,24},{24,32},{32,40},{40,48},{48,56},{56,64},{64,7... | collective-permute-start | bytes 44 | tf_op jit(solution)/shard_map/ppermute | solution.py:15
  54.3 7.8 %collective-permute-start.9 = (s32[3]{0:T(128)S(1)}, s32[3]{0:T(128)S(1)}, u32[]{:S(2)}, u32[]{:S(2)}) collective-permute-start(s32[3]{0:T(128)S(1)} %get-tuple-element.172), channel_id=1, source_target_pairs={{0,8},{8,16},{16,24},{24,32},{32,40},{40,48},{48,56},{56,64},{64,7... | collective-permute-start | bytes 44 | tf_op jit(solution)/shard_map/ppermute | solution.py:15
  66.2 130.9 %copy-start.6 = (f32[1,8]{1,0:T(1,128)S(1)}, f32[1,8]{1,0:T(1,128)}, u32[]{:S(2)}) copy-start(f32[1,8]{1,0:T(1,128)} %param.29) | copy-start | bytes 100
  66.3 6.9 collective-permute-start
  73.3 6.9 collective-permute-start
  80.3 6.9 collective-permute-start
  87.3 7.8 %collective-permute-start = (bf16[8,64,64]{2,1,0:T(8,128)(2,1)S(1)}, bf16[8,64,64]{2,1,0:T(8,128)(2,1)S(1)}, u32[]{:S(2)}, u32[]{:S(2)}) collective-permute-start(bf16[8,64,64]{2,1,0:T(8,128)(2,1)S(1)} %fusion.132), channel_id=1, source_target_pairs={{0,8},{8,16},{16,24},{24,32},{32,40},{40,48},{48,56},{56,64},{64,7... | collective-permute-start | bytes 196616 | tf_op jit(solution)/shard_map/while/body/eval_jaxpr/ppermute | solution.py:15
  95.2 9.0 %collective-permute-start = (bf16[8,64,64]{2,1,0:T(8,128)(2,1)S(1)}, bf16[8,64,64]{2,1,0:T(8,128)(2,1)S(1)}, u32[]{:S(2)}, u32[]{:S(2)}) collective-permute-start(bf16[8,64,64]{2,1,0:T(8,128)(2,1)S(1)} %fusion.132), channel_id=1, source_target_pairs={{0,8},{8,16},{16,24},{24,32},{32,40},{40,48},{48,56},{56,64},{64,7... | collective-permute-start | bytes 196616 | tf_op jit(solution)/shard_map/while/body/eval_jaxpr/ppermute | solution.py:15
  104.4 9.0 %collective-permute-start = (bf16[8,64,64]{2,1,0:T(8,128)(2,1)S(1)}, bf16[8,64,64]{2,1,0:T(8,128)(2,1)S(1)}, u32[]{:S(2)}, u32[]{:S(2)}) collective-permute-start(bf16[8,64,64]{2,1,0:T(8,128)(2,1)S(1)} %fusion.132), channel_id=1, source_target_pairs={{0,8},{8,16},{16,24},{24,32},{32,40},{40,48},{48,56},{56,64},{64,7... | collective-permute-start | bytes 196616 | tf_op jit(solution)/shard_map/while/body/eval_jaxpr/ppermute | solution.py:15
  113.5 9.0 %collective-permute-start = (bf16[8,64,64]{2,1,0:T(8,128)(2,1)S(1)}, bf16[8,64,64]{2,1,0:T(8,128)(2,1)S(1)}, u32[]{:S(2)}, u32[]{:S(2)}) collective-permute-start(bf16[8,64,64]{2,1,0:T(8,128)(2,1)S(1)} %fusion.132), channel_id=1, source_target_pairs={{0,8},{8,16},{16,24},{24,32},{32,40},{40,48},{48,56},{56,64},{64,7... | collective-permute-start | bytes 196616 | tf_op jit(solution)/shard_map/while/body/eval_jaxpr/ppermute | solution.py:15
  122.6 9.2 %collective-permute-start = (bf16[8,64,64]{2,1,0:T(8,128)(2,1)S(1)}, bf16[8,64,64]{2,1,0:T(8,128)(2,1)S(1)}, u32[]{:S(2)}, u32[]{:S(2)}) collective-permute-start(bf16[8,64,64]{2,1,0:T(8,128)(2,1)S(1)} %fusion.132), channel_id=1, source_target_pairs={{0,8},{8,16},{16,24},{24,32},{32,40},{40,48},{48,56},{56,64},{64,7... | collective-permute-start | bytes 196616 | tf_op jit(solution)/shard_map/while/body/eval_jaxpr/ppermute | solution.py:15
  132.0 10.6 %collective-permute-start = (bf16[8,64,64]{2,1,0:T(8,128)(2,1)S(1)}, bf16[8,64,64]{2,1,0:T(8,128)(2,1)S(1)}, u32[]{:S(2)}, u32[]{:S(2)}) collective-permute-start(bf16[8,64,64]{2,1,0:T(8,128)(2,1)S(1)} %fusion.132), channel_id=1, source_target_pairs={{0,8},{8,16},{16,24},{24,32},{32,40},{40,48},{48,56},{56,64},{64,7... | collective-permute-start | bytes 196616 | tf_op jit(solution)/shard_map/while/body/eval_jaxpr/ppermute | solution.py:15
  142.7 9.1 %collective-permute-start = (bf16[8,64,64]{2,1,0:T(8,128)(2,1)S(1)}, bf16[8,64,64]{2,1,0:T(8,128)(2,1)S(1)}, u32[]{:S(2)}, u32[]{:S(2)}) collective-permute-start(bf16[8,64,64]{2,1,0:T(8,128)(2,1)S(1)} %fusion.132), channel_id=1, source_target_pairs={{0,8},{8,16},{16,24},{24,32},{32,40},{40,48},{48,56},{56,64},{64,7... | collective-permute-start | bytes 196616 | tf_op jit(solution)/shard_map/while/body/eval_jaxpr/ppermute | solution.py:15
  152.0 8.5 %collective-permute-start = (bf16[8,64,64]{2,1,0:T(8,128)(2,1)S(1)}, bf16[8,64,64]{2,1,0:T(8,128)(2,1)S(1)}, u32[]{:S(2)}, u32[]{:S(2)}) collective-permute-start(bf16[8,64,64]{2,1,0:T(8,128)(2,1)S(1)} %fusion.132), channel_id=1, source_target_pairs={{0,8},{8,16},{16,24},{24,32},{32,40},{40,48},{48,56},{56,64},{64,7... | collective-permute-start | bytes 196616 | tf_op jit(solution)/shard_map/while/body/eval_jaxpr/ppermute | solution.py:15
  160.7 9.0 %collective-permute-start = (bf16[8,64,64]{2,1,0:T(8,128)(2,1)S(1)}, bf16[8,64,64]{2,1,0:T(8,128)(2,1)S(1)}, u32[]{:S(2)}, u32[]{:S(2)}) collective-permute-start(bf16[8,64,64]{2,1,0:T(8,128)(2,1)S(1)} %fusion.132), channel_id=1, source_target_pairs={{0,8},{8,16},{16,24},{24,32},{32,40},{40,48},{48,56},{56,64},{64,7... | collective-permute-start | bytes 196616 | tf_op jit(solution)/shard_map/while/body/eval_jaxpr/ppermute | solution.py:15
  169.8 9.0 %collective-permute-start = (bf16[8,64,64]{2,1,0:T(8,128)(2,1)S(1)}, bf16[8,64,64]{2,1,0:T(8,128)(2,1)S(1)}, u32[]{:S(2)}, u32[]{:S(2)}) collective-permute-start(bf16[8,64,64]{2,1,0:T(8,128)(2,1)S(1)} %fusion.132), channel_id=1, source_target_pairs={{0,8},{8,16},{16,24},{24,32},{32,40},{40,48},{48,56},{56,64},{64,7... | collective-permute-start | bytes 196616 | tf_op jit(solution)/shard_map/while/body/eval_jaxpr/ppermute | solution.py:15
  178.9 9.0 %collective-permute-start = (bf16[8,64,64]{2,1,0:T(8,128)(2,1)S(1)}, bf16[8,64,64]{2,1,0:T(8,128)(2,1)S(1)}, u32[]{:S(2)}, u32[]{:S(2)}) collective-permute-start(bf16[8,64,64]{2,1,0:T(8,128)(2,1)S(1)} %fusion.132), channel_id=1, source_target_pairs={{0,8},{8,16},{16,24},{24,32},{32,40},{40,48},{48,56},{56,64},{64,7... | collective-permute-start | bytes 196616 | tf_op jit(solution)/shard_map/while/body/eval_jaxpr/ppermute | solution.py:15
  188.1 9.0 %collective-permute-start = (bf16[8,64,64]{2,1,0:T(8,128)(2,1)S(1)}, bf16[8,64,64]{2,1,0:T(8,128)(2,1)S(1)}, u32[]{:S(2)}, u32[]{:S(2)}) collective-permute-start(bf16[8,64,64]{2,1,0:T(8,128)(2,1)S(1)} %fusion.132), channel_id=1, source_target_pairs={{0,8},{8,16},{16,24},{24,32},{32,40},{40,48},{48,56},{56,64},{64,7... | collective-permute-start | bytes 196616 | tf_op jit(solution)/shard_map/while/body/eval_jaxpr/ppermute | solution.py:15
  213.9 48.7 %copy-start.2 = (bf16[2,128,448]{1,2,0:T(8,128)(2,1)S(1)}, bf16[2,128,448]{1,2,0:T(8,128)(2,1)}, u32[]{:S(2)}) copy-start(bf16[2,128,448]{1,2,0:T(8,128)(2,1)} %param.19) | copy-start | bytes 688132
  218.5 287.9 %reduce-scatter.6.cloned.1.call-start = ((), (), s32[]{:S(2)}) async-start(), calls=%async_computation.4 | async-start | bytes 1032192 | tf_op jit(solution)/shard_map/reduce_scatter | solution.py:122
  218.6 7.7 %collective-permute-start.6 = (s32[3]{0:T(128)S(1)}, s32[3]{0:T(128)S(1)}, u32[]{:S(2)}, u32[]{:S(2)}) collective-permute-start(s32[3]{0:T(128)S(1)} %slice.224), channel_id=1, source_target_pairs={{0,8},{8,16},{16,24},{24,32},{32,40},{40,48},{48,56},{56,64},{64,7... | collective-permute-start | bytes 44 | tf_op jit(solution)/shard_map/ppermute | solution.py:15
  263.5 2.6 collective-permute-start.5
  300.5 5.6 collective-permute-start.7
  307.5 6.9 collective-permute-start.1
  314.5 6.9 collective-permute-start.1
  321.5 7.6 %collective-permute-start.1 = (bf16[8,64,64]{2,1,0:T(8,128)(2,1)S(1)}, bf16[8,64,64]{2,1,0:T(8,128)(2,1)S(1)}, u32[]{:S(2)}, u32[]{:S(2)}) collective-permute-start(bf16[8,64,64]{2,1,0:T(8,128)(2,1)S(1)} %fusion.133), channel_id=1, source_target_pairs={{0,8},{8,16},{16,24},{24,32},{32,40},{40,48},{48,56},{56,64},{64,7... | collective-permute-start | bytes 196616 | tf_op jit(solution)/shard_map/while/body/eval_jaxpr/ppermute | solution.py:15
  329.3 8.8 %collective-permute-start.1 = (bf16[8,64,64]{2,1,0:T(8,128)(2,1)S(1)}, bf16[8,64,64]{2,1,0:T(8,128)(2,1)S(1)}, u32[]{:S(2)}, u32[]{:S(2)}) collective-permute-start(bf16[8,64,64]{2,1,0:T(8,128)(2,1)S(1)} %fusion.133), channel_id=1, source_target_pairs={{0,8},{8,16},{16,24},{24,32},{32,40},{40,48},{48,56},{56,64},{64,7... | collective-permute-start | bytes 196616 | tf_op jit(solution)/shard_map/while/body/eval_jaxpr/ppermute | solution.py:15
  338.2 9.0 %collective-permute-start.1 = (bf16[8,64,64]{2,1,0:T(8,128)(2,1)S(1)}, bf16[8,64,64]{2,1,0:T(8,128)(2,1)S(1)}, u32[]{:S(2)}, u32[]{:S(2)}) collective-permute-start(bf16[8,64,64]{2,1,0:T(8,128)(2,1)S(1)} %fusion.133), channel_id=1, source_target_pairs={{0,8},{8,16},{16,24},{24,32},{32,40},{40,48},{48,56},{56,64},{64,7... | collective-permute-start | bytes 196616 | tf_op jit(solution)/shard_map/while/body/eval_jaxpr/ppermute | solution.py:15
  347.4 9.0 %collective-permute-start.1 = (bf16[8,64,64]{2,1,0:T(8,128)(2,1)S(1)}, bf16[8,64,64]{2,1,0:T(8,128)(2,1)S(1)}, u32[]{:S(2)}, u32[]{:S(2)}) collective-permute-start(bf16[8,64,64]{2,1,0:T(8,128)(2,1)S(1)} %fusion.133), channel_id=1, source_target_pairs={{0,8},{8,16},{16,24},{24,32},{32,40},{40,48},{48,56},{56,64},{64,7... | collective-permute-start | bytes 196616 | tf_op jit(solution)/shard_map/while/body/eval_jaxpr/ppermute | solution.py:15
  356.5 9.0 %collective-permute-start.1 = (bf16[8,64,64]{2,1,0:T(8,128)(2,1)S(1)}, bf16[8,64,64]{2,1,0:T(8,128)(2,1)S(1)}, u32[]{:S(2)}, u32[]{:S(2)}) collective-permute-start(bf16[8,64,64]{2,1,0:T(8,128)(2,1)S(1)} %fusion.133), channel_id=1, source_target_pairs={{0,8},{8,16},{16,24},{24,32},{32,40},{40,48},{48,56},{56,64},{64,7... | collective-permute-start | bytes 196616 | tf_op jit(solution)/shard_map/while/body/eval_jaxpr/ppermute | solution.py:15
  365.6 9.2 %collective-permute-start.1 = (bf16[8,64,64]{2,1,0:T(8,128)(2,1)S(1)}, bf16[8,64,64]{2,1,0:T(8,128)(2,1)S(1)}, u32[]{:S(2)}, u32[]{:S(2)}) collective-permute-start(bf16[8,64,64]{2,1,0:T(8,128)(2,1)S(1)} %fusion.133), channel_id=1, source_target_pairs={{0,8},{8,16},{16,24},{24,32},{32,40},{40,48},{48,56},{56,64},{64,7... | collective-permute-start | bytes 196616 | tf_op jit(solution)/shard_map/while/body/eval_jaxpr/ppermute | solution.py:15
  375.0 10.6 %collective-permute-start.1 = (bf16[8,64,64]{2,1,0:T(8,128)(2,1)S(1)}, bf16[8,64,64]{2,1,0:T(8,128)(2,1)S(1)}, u32[]{:S(2)}, u32[]{:S(2)}) collective-permute-start(bf16[8,64,64]{2,1,0:T(8,128)(2,1)S(1)} %fusion.133), channel_id=1, source_target_pairs={{0,8},{8,16},{16,24},{24,32},{32,40},{40,48},{48,56},{56,64},{64,7... | collective-permute-start | bytes 196616 | tf_op jit(solution)/shard_map/while/body/eval_jaxpr/ppermute | solution.py:15
  385.7 9.1 %collective-permute-start.1 = (bf16[8,64,64]{2,1,0:T(8,128)(2,1)S(1)}, bf16[8,64,64]{2,1,0:T(8,128)(2,1)S(1)}, u32[]{:S(2)}, u32[]{:S(2)}) collective-permute-start(bf16[8,64,64]{2,1,0:T(8,128)(2,1)S(1)} %fusion.133), channel_id=1, source_target_pairs={{0,8},{8,16},{16,24},{24,32},{32,40},{40,48},{48,56},{56,64},{64,7... | collective-permute-start | bytes 196616 | tf_op jit(solution)/shard_map/while/body/eval_jaxpr/ppermute | solution.py:15
  395.0 8.5 %collective-permute-start.1 = (bf16[8,64,64]{2,1,0:T(8,128)(2,1)S(1)}, bf16[8,64,64]{2,1,0:T(8,128)(2,1)S(1)}, u32[]{:S(2)}, u32[]{:S(2)}) collective-permute-start(bf16[8,64,64]{2,1,0:T(8,128)(2,1)S(1)} %fusion.133), channel_id=1, source_target_pairs={{0,8},{8,16},{16,24},{24,32},{32,40},{40,48},{48,56},{56,64},{64,7... | collective-permute-start | bytes 196616 | tf_op jit(solution)/shard_map/while/body/eval_jaxpr/ppermute | solution.py:15
  403.7 9.0 %collective-permute-start.1 = (bf16[8,64,64]{2,1,0:T(8,128)(2,1)S(1)}, bf16[8,64,64]{2,1,0:T(8,128)(2,1)S(1)}, u32[]{:S(2)}, u32[]{:S(2)}) collective-permute-start(bf16[8,64,64]{2,1,0:T(8,128)(2,1)S(1)} %fusion.133), channel_id=1, source_target_pairs={{0,8},{8,16},{16,24},{24,32},{32,40},{40,48},{48,56},{56,64},{64,7... | collective-permute-start | bytes 196616 | tf_op jit(solution)/shard_map/while/body/eval_jaxpr/ppermute | solution.py:15
  412.9 9.0 %collective-permute-start.1 = (bf16[8,64,64]{2,1,0:T(8,128)(2,1)S(1)}, bf16[8,64,64]{2,1,0:T(8,128)(2,1)S(1)}, u32[]{:S(2)}, u32[]{:S(2)}) collective-permute-start(bf16[8,64,64]{2,1,0:T(8,128)(2,1)S(1)} %fusion.133), channel_id=1, source_target_pairs={{0,8},{8,16},{16,24},{24,32},{32,40},{40,48},{48,56},{56,64},{64,7... | collective-permute-start | bytes 196616 | tf_op jit(solution)/shard_map/while/body/eval_jaxpr/ppermute | solution.py:15
  422.0 9.0 %collective-permute-start.1 = (bf16[8,64,64]{2,1,0:T(8,128)(2,1)S(1)}, bf16[8,64,64]{2,1,0:T(8,128)(2,1)S(1)}, u32[]{:S(2)}, u32[]{:S(2)}) collective-permute-start(bf16[8,64,64]{2,1,0:T(8,128)(2,1)S(1)} %fusion.133), channel_id=1, source_target_pairs={{0,8},{8,16},{16,24},{24,32},{32,40},{40,48},{48,56},{56,64},{64,7... | collective-permute-start | bytes 196616 | tf_op jit(solution)/shard_map/while/body/eval_jaxpr/ppermute | solution.py:15
  431.1 9.0 %collective-permute-start.1 = (bf16[8,64,64]{2,1,0:T(8,128)(2,1)S(1)}, bf16[8,64,64]{2,1,0:T(8,128)(2,1)S(1)}, u32[]{:S(2)}, u32[]{:S(2)}) collective-permute-start(bf16[8,64,64]{2,1,0:T(8,128)(2,1)S(1)} %fusion.133), channel_id=1, source_target_pairs={{0,8},{8,16},{16,24},{24,32},{32,40},{40,48},{48,56},{56,64},{64,7... | collective-permute-start | bytes 196616 | tf_op jit(solution)/shard_map/while/body/eval_jaxpr/ppermute | solution.py:15
  461.3 75.8 %copy-start.10 = (bf16[1,3584,8]{1,2,0:T(8,128)(2,1)S(1)}, bf16[1,3584,8]{1,2,0:T(8,128)(2,1)}, u32[]{:S(2)}) copy-start(bf16[1,3584,8]{1,2,0:T(8,128)(2,1)} %param.24) | copy-start | bytes 172036
  461.3 288.9 %reduce-scatter.8.cloned.1.call-start = ((), (), s32[]{:S(2)}) async-start(), calls=%async_computation.5 | async-start | bytes 1032192 | tf_op jit(solution)/shard_map/reduce_scatter | solution.py:122
  507.3 2.7 collective-permute-start.8
  544.2 5.6 collective-permute-start.10
  551.2 6.9 collective-permute-start.2
  558.2 6.9 collective-permute-start.2
  565.2 7.2 collective-permute-start.2
  572.6 9.0 %collective-permute-start.2 = (bf16[8,64,64]{2,1,0:T(8,128)(2,1)S(1)}, bf16[8,64,64]{2,1,0:T(8,128)(2,1)S(1)}, u32[]{:S(2)}, u32[]{:S(2)}) collective-permute-start(bf16[8,64,64]{2,1,0:T(8,128)(2,1)S(1)} %fusion.134), channel_id=1, source_target_pairs={{0,8},{8,16},{16,24},{24,32},{32,40},{40,48},{48,56},{56,64},{64,7... | collective-permute-start | bytes 196616 | tf_op jit(solution)/shard_map/while/body/eval_jaxpr/ppermute | solution.py:15
  581.7 9.0 %collective-permute-start.2 = (bf16[8,64,64]{2,1,0:T(8,128)(2,1)S(1)}, bf16[8,64,64]{2,1,0:T(8,128)(2,1)S(1)}, u32[]{:S(2)}, u32[]{:S(2)}) collective-permute-start(bf16[8,64,64]{2,1,0:T(8,128)(2,1)S(1)} %fusion.134), channel_id=1, source_target_pairs={{0,8},{8,16},{16,24},{24,32},{32,40},{40,48},{48,56},{56,64},{64,7... | collective-permute-start | bytes 196616 | tf_op jit(solution)/shard_map/while/body/eval_jaxpr/ppermute | solution.py:15
  590.9 9.0 %collective-permute-start.2 = (bf16[8,64,64]{2,1,0:T(8,128)(2,1)S(1)}, bf16[8,64,64]{2,1,0:T(8,128)(2,1)S(1)}, u32[]{:S(2)}, u32[]{:S(2)}) collective-permute-start(bf16[8,64,64]{2,1,0:T(8,128)(2,1)S(1)} %fusion.134), channel_id=1, source_target_pairs={{0,8},{8,16},{16,24},{24,32},{32,40},{40,48},{48,56},{56,64},{64,7... | collective-permute-start | bytes 196616 | tf_op jit(solution)/shard_map/while/body/eval_jaxpr/ppermute | solution.py:15
  600.0 9.0 %collective-permute-start.2 = (bf16[8,64,64]{2,1,0:T(8,128)(2,1)S(1)}, bf16[8,64,64]{2,1,0:T(8,128)(2,1)S(1)}, u32[]{:S(2)}, u32[]{:S(2)}) collective-permute-start(bf16[8,64,64]{2,1,0:T(8,128)(2,1)S(1)} %fusion.134), channel_id=1, source_target_pairs={{0,8},{8,16},{16,24},{24,32},{32,40},{40,48},{48,56},{56,64},{64,7... | collective-permute-start | bytes 196616 | tf_op jit(solution)/shard_map/while/body/eval_jaxpr/ppermute | solution.py:15
  609.1 9.4 %collective-permute-start.2 = (bf16[8,64,64]{2,1,0:T(8,128)(2,1)S(1)}, bf16[8,64,64]{2,1,0:T(8,128)(2,1)S(1)}, u32[]{:S(2)}, u32[]{:S(2)}) collective-permute-start(bf16[8,64,64]{2,1,0:T(8,128)(2,1)S(1)} %fusion.134), channel_id=1, source_target_pairs={{0,8},{8,16},{16,24},{24,32},{32,40},{40,48},{48,56},{56,64},{64,7... | collective-permute-start | bytes 196616 | tf_op jit(solution)/shard_map/while/body/eval_jaxpr/ppermute | solution.py:15
  618.6 10.4 %collective-permute-start.2 = (bf16[8,64,64]{2,1,0:T(8,128)(2,1)S(1)}, bf16[8,64,64]{2,1,0:T(8,128)(2,1)S(1)}, u32[]{:S(2)}, u32[]{:S(2)}) collective-permute-start(bf16[8,64,64]{2,1,0:T(8,128)(2,1)S(1)} %fusion.134), channel_id=1, source_target_pairs={{0,8},{8,16},{16,24},{24,32},{32,40},{40,48},{48,56},{56,64},{64,7... | collective-permute-start | bytes 196616 | tf_op jit(solution)/shard_map/while/body/eval_jaxpr/ppermute | solution.py:15
  629.2 9.0 %collective-permute-start.2 = (bf16[8,64,64]{2,1,0:T(8,128)(2,1)S(1)}, bf16[8,64,64]{2,1,0:T(8,128)(2,1)S(1)}, u32[]{:S(2)}, u32[]{:S(2)}) collective-permute-start(bf16[8,64,64]{2,1,0:T(8,128)(2,1)S(1)} %fusion.134), channel_id=1, source_target_pairs={{0,8},{8,16},{16,24},{24,32},{32,40},{40,48},{48,56},{56,64},{64,7... | collective-permute-start | bytes 196616 | tf_op jit(solution)/shard_map/while/body/eval_jaxpr/ppermute | solution.py:15
  638.3 8.7 %collective-permute-start.2 = (bf16[8,64,64]{2,1,0:T(8,128)(2,1)S(1)}, bf16[8,64,64]{2,1,0:T(8,128)(2,1)S(1)}, u32[]{:S(2)}, u32[]{:S(2)}) collective-permute-start(bf16[8,64,64]{2,1,0:T(8,128)(2,1)S(1)} %fusion.134), channel_id=1, source_target_pairs={{0,8},{8,16},{16,24},{24,32},{32,40},{40,48},{48,56},{56,64},{64,7... | collective-permute-start | bytes 196616 | tf_op jit(solution)/shard_map/while/body/eval_jaxpr/ppermute | solution.py:15
  647.2 9.0 %collective-permute-start.2 = (bf16[8,64,64]{2,1,0:T(8,128)(2,1)S(1)}, bf16[8,64,64]{2,1,0:T(8,128)(2,1)S(1)}, u32[]{:S(2)}, u32[]{:S(2)}) collective-permute-start(bf16[8,64,64]{2,1,0:T(8,128)(2,1)S(1)} %fusion.134), channel_id=1, source_target_pairs={{0,8},{8,16},{16,24},{24,32},{32,40},{40,48},{48,56},{56,64},{64,7... | collective-permute-start | bytes 196616 | tf_op jit(solution)/shard_map/while/body/eval_jaxpr/ppermute | solution.py:15
  656.3 9.0 %collective-permute-start.2 = (bf16[8,64,64]{2,1,0:T(8,128)(2,1)S(1)}, bf16[8,64,64]{2,1,0:T(8,128)(2,1)S(1)}, u32[]{:S(2)}, u32[]{:S(2)}) collective-permute-start(bf16[8,64,64]{2,1,0:T(8,128)(2,1)S(1)} %fusion.134), channel_id=1, source_target_pairs={{0,8},{8,16},{16,24},{24,32},{32,40},{40,48},{48,56},{56,64},{64,7... | collective-permute-start | bytes 196616 | tf_op jit(solution)/shard_map/while/body/eval_jaxpr/ppermute | solution.py:15
  665.4 9.0 %collective-permute-start.2 = (bf16[8,64,64]{2,1,0:T(8,128)(2,1)S(1)}, bf16[8,64,64]{2,1,0:T(8,128)(2,1)S(1)}, u32[]{:S(2)}, u32[]{:S(2)}) collective-permute-start(bf16[8,64,64]{2,1,0:T(8,128)(2,1)S(1)} %fusion.134), channel_id=1, source_target_pairs={{0,8},{8,16},{16,24},{24,32},{32,40},{40,48},{48,56},{56,64},{64,7... | collective-permute-start | bytes 196616 | tf_op jit(solution)/shard_map/while/body/eval_jaxpr/ppermute | solution.py:15
  674.6 9.0 %collective-permute-start.2 = (bf16[8,64,64]{2,1,0:T(8,128)(2,1)S(1)}, bf16[8,64,64]{2,1,0:T(8,128)(2,1)S(1)}, u32[]{:S(2)}, u32[]{:S(2)}) collective-permute-start(bf16[8,64,64]{2,1,0:T(8,128)(2,1)S(1)} %fusion.134), channel_id=1, source_target_pairs={{0,8},{8,16},{16,24},{24,32},{32,40},{40,48},{48,56},{56,64},{64,7... | collective-permute-start | bytes 196616 | tf_op jit(solution)/shard_map/while/body/eval_jaxpr/ppermute | solution.py:15
  (5 other events, 42.6 us)
Sparse Core Ops, SparseCore 0:
  218.6 43.9 reduce-scatter.3
  461.4 44.9 reduce-scatter.5
  705.0 45.1 reduce-scatter.7
where the time goes:
time: 760 us; the launch traced here: 758 us
  starting transfers between devices  291 us (38%)
  waiting for transfers between devices  254 us (33%)
  blocking collectives  132 us (17%)
  matrix products  34.3 us (5%)
  other arithmetic  18.3 us (2%)
  between operations  17.5 us (2%)
  local copies, waits for them, and re-layouts  10.9 us (1%)
    ppermute x53, starting transfers between devices, shifted(): return lax.ppermute(block, axis, route)  291 us
    ppermute x53, waiting for transfers between devices, shifted(): return lax.ppermute(block, axis, route)  129 us
    reduce_scatter x3, waiting for transfers between devices, mixer_layer(): lax.psum_scatter(update.astype(jnp.bfloat16), 'mp', scatter_dimension=1,...  125 us
    all_gather x3, blocking collectives, mixer_layer(): whole = lax.all_gather(hidden_rows, 'mp', axis=1, tiled=True)  83.3 us
    psum x3, blocking collectives, mixer_layer(): squares = lax.psum(jnp.sum(gated * gated, axis=-1), 'mp')  48.2 us
  transfers between devices with their start and end apart: 56, of which 51 were waited for; matrix products, arithmetic and copies ran while one was open for 1% of the time, Pallas kernels for 0%

commit v1 on v0

--- a/solution.py
+++ b/solution.py
@@ -73,7 +73,9 @@
     inner_gain,
     out_weight,
 ):
-    whole = lax.all_gather(hidden_rows, "mp", axis=1, tiled=True)
+    whole = jnp.concatenate(
+        lax.all_to_all(jnp.stack([hidden_rows] * lax.axis_size("mp")), "mp", 0, 0), axis=1
+    )
     normed = norm_rows(whole, norm_gain)
     width_loc = in_weight.shape[-1]
     both = jnp.dot(

time: 760 us -> 753 us (level)
  blocking collectives: 132 us -> 46.1 us
  waiting for transfers between devices: 254 us -> 315 us
  starting transfers between devices: 291 us -> 303 us
    all_gather x3 -> x0, blocking collectives: 83.3 us -> none  [mixer_layer(): whole = lax.all_gather(hidden_rows, 'mp', axis=1, tiled=True)]
    all_to_all x0 -> x3, waiting for transfers between devices: none -> 47.1 us  [mixer_layer(): lax.all_to_all(jnp.stack([hidden_rows] * lax.axis_size('mp')), 'mp', 0, 0)]
    all_to_all x0 -> x3, starting transfers between devices: none -> 17.2 us  [mixer_layer(): lax.all_to_all(jnp.stack([hidden_rows] * lax.axis_size('mp')), 'mp', 0, 0)]
  transfers between devices with their start and end apart: 56 -> 59, of which waited for: 51 -> 57; matrix products, arithmetic and copies ran while one was open for 1% -> 2% of each run, Pallas kernels for 0% -> 0%
where the time goes in v1:
time: 753 us; the launch traced here: 751 us
  waiting for transfers between devices  315 us (42%)
  starting transfers between devices  303 us (40%)
  blocking collectives  46.1 us (6%)
  matrix products  32 us (4%)
  other arithmetic  20 us (3%)
  between operations  17.6 us (2%)
  local copies, waits for them, and re-layouts  16.3 us (2%)
    ppermute x53, starting transfers between devices, shifted(): return lax.ppermute(block, axis, route)  285 us
    ppermute x53, waiting for transfers between devices, shifted(): return lax.ppermute(block, axis, route)  136 us
    reduce_scatter x3, waiting for transfers between devices, mixer_layer(): lax.psum_scatter(update.astype(jnp.bfloat16), 'mp', scatter_dimension=1,...  132 us
    all_to_all x3, waiting for transfers between devices, mixer_layer(): lax.all_to_all(jnp.stack([hidden_rows] * lax.axis_size('mp')), 'mp', 0, 0)  47.1 us
    psum x3, blocking collectives, mixer_layer(): squares = lax.psum(jnp.sum(gated * gated, axis=-1), 'mp')  46.1 us
    all_to_all x3, starting transfers between devices, mixer_layer(): lax.all_to_all(jnp.stack([hidden_rows] * lax.axis_size('mp')), 'mp', 0, 0)  17.2 us
  transfers between devices with their start and end apart: 59, of which 57 were waited for; matrix products, arithmetic and copies ran while one was open for 2% of the time, Pallas kernels for 0%

profile of v1, /device:TPU:2, one launch (start us, length us, event | category | flops | bytes accessed | tf_op | source)
XLA Modules:
  0.0 750.9 jit_solution(9121572691785536222)
XLA Ops:
  8.6 8.5 %all-to-all-start = ((bf16[8,128,448]{1,2,0:T(8,128)(2,1)}), bf16[8,128,448]{1,2,0:T(8,128)(2,1)S(1)}, u32[]{:S(2)}, u32[]{:S(2)}) async-start(bf16[8,128,448]{1,2,0:T(8,128)(2,1)} %stack.12), calls=%async_computation | async-start | bytes 1835008 | tf_op jit(solution)/shard_map/all_to_all | solution.py:77
  23.8 8.4 %copy.83 = bf16[448,8,2,512]{3,1,2,0:T(8,128)(2,1)} copy(bf16[448,8,2,512]{3,2,1,0:T(2,128)(2,1)} %bitcast.180) | data formatting | bytes 14680064
  38.4 4.5 all-to-all-done
  44.6 4.2 fusion.107
  56.2 132.2 %while.33 = (s32[]{:T(128)}, f32[8,64,64]{2,1,0:T(8,128)S(1)}, f32[8]{0:T(128)S(1)}, f32[8,64,64]{2,1,0:T(8,128)S(1)}, s32[]{:T(128)}, /*index=5*/s32[]{:T(128)}) while((s32[]{:T(128)}, f32[8,64,64]{2,1,0:T(8,128)S(1)}, f32[8]{0:T(128)S(1)}, f32[8,64,64]{2,1,0:T(8,128)S(1)}, s32[]{:T(128)}, /*index=5*/s32[]{:T(128)}) %tuple.86), condition=%wide.region_3.4_spmd.clone, body=%wide.region_2.3_spmd.clone.sunk | while | flops 163843 | bytes 786583 | solution.py:110
  77.4 5.4 collective-permute-start
  85.4 6.5 collective-permute-start
  94.5 6.5 collective-permute-start
  104.3 6.9 collective-permute-start
  114.8 6.6 collective-permute-start
  124.0 6.3 collective-permute-start
  132.9 6.5 collective-permute-start
  142.1 6.5 collective-permute-start
  151.2 6.5 collective-permute-start
  160.3 6.5 collective-permute-start
  169.7 6.8 collective-permute-start
  179.1 6.8 collective-permute-start
  189.1 15.7 %psum.21 = f32[128]{0:T(128)S(1)} all-reduce(f32[128]{0:T(128)S(1)} %multiply_reduce_fusion.2), channel_id=1, replica_groups=mesh['section'=2,'seq'=16,'mp'=8] {'mp'}, use_global_device_ids=true, to_apply=%region_5.6 | all-reduce | flops 128 | bytes 1024 | tf_op jit(solution)/shard_map/psum | solution.py:120
  204.8 4.6 convolution_convert_fusion.2
  209.5 43.8 %reduce-scatter.4.cloned.1.call-done = bf16[128,448]{0,1:T(8,128)(2,1)} async-done(((bf16[128,3584]{0,1:T(8,128)(2,1)}), bf16[128,448]{0,1:T(8,128)(2,1)}) %reduce-scatter.4.cloned.1.call-update) | async-done | bytes 114704 | tf_op jit(solution)/shard_map/reduce_scatter | solution.py:124
  257.6 4.4 all-to-all-start.1
  262.1 3.5 collective-permute-start.6
  270.9 17.4 %all-to-all-done.1 = bf16[8,128,448]{1,2,0:T(8,128)(2,1)S(1)} async-done(((bf16[8,128,448]{1,2,0:T(8,128)(2,1)}), bf16[8,128,448]{1,2,0:T(8,128)(2,1)S(1)}, u32[]{:S(2)}, u32[]{:S(2)}) %all-to-all-start.1) | async-done | bytes 917536 | tf_op jit(solution)/shard_map/all_to_all | solution.py:77
  290.0 4.2 fusion.108
  301.6 132.1 %while.34 = (s32[]{:T(128)}, f32[8,64,64]{2,1,0:T(8,128)S(1)}, f32[8]{0:T(128)S(1)}, f32[8,64,64]{2,1,0:T(8,128)S(1)}, s32[]{:T(128)}, /*index=5*/s32[]{:T(128)}) while((s32[]{:T(128)}, f32[8,64,64]{2,1,0:T(8,128)S(1)}, f32[8]{0:T(128)S(1)}, f32[8,64,64]{2,1,0:T(8,128)S(1)}, s32[]{:T(128)}, /*index=5*/s32[]{:T(128)}) %tuple.89), condition=%wide.region_10.11_spmd.clone, body=%wide.region_9.10_spmd.clone.sunk | while | flops 163843 | bytes 786583 | solution.py:110
  305.1 3.5 collective-permute-done.1
  312.1 3.5 collective-permute-done.1
  319.1 3.5 collective-permute-done.1
  322.7 5.3 collective-permute-start.1
  330.7 6.5 collective-permute-start.1
  339.8 6.5 collective-permute-start.1
  349.6 6.8 collective-permute-start.1
  360.0 6.5 collective-permute-start.1
  369.2 6.3 collective-permute-start.1
  378.2 6.5 collective-permute-start.1
  387.3 6.5 collective-permute-start.1
  396.4 6.5 collective-permute-start.1
  405.6 6.5 collective-permute-start.1
  414.9 6.8 collective-permute-start.1
  424.4 6.8 collective-permute-start.1
  434.3 15.2 %psum.22 = f32[128]{0:T(128)S(1)} all-reduce(f32[128]{0:T(128)S(1)} %multiply_reduce_fusion.1), channel_id=1, replica_groups=mesh['section'=2,'seq'=16,'mp'=8] {'mp'}, use_global_device_ids=true, to_apply=%region_12.13 | all-reduce | flops 128 | bytes 1024 | tf_op jit(solution)/shard_map/psum | solution.py:120
  449.6 4.6 convolution_convert_fusion.1
  454.2 43.9 %reduce-scatter.6.cloned.1.call-done = bf16[128,448]{0,1:T(8,128)(2,1)} async-done(((bf16[128,3584]{0,1:T(8,128)(2,1)}), bf16[128,448]{0,1:T(8,128)(2,1)}) %reduce-scatter.6.cloned.1.call-update) | async-done | bytes 114704 | tf_op jit(solution)/shard_map/reduce_scatter | solution.py:124
  502.3 4.3 all-to-all-start.2
  508.0 25.1 %all-to-all-done.2 = bf16[8,128,448]{1,2,0:T(8,128)(2,1)S(1)} async-done(((bf16[8,128,448]{1,2,0:T(8,128)(2,1)}), bf16[8,128,448]{1,2,0:T(8,128)(2,1)S(1)}, u32[]{:S(2)}, u32[]{:S(2)}) %all-to-all-start.2) | async-done | bytes 917536 | tf_op jit(solution)/shard_map/all_to_all | solution.py:77
  534.7 4.2 fusion.109
  546.3 132.1 %while.35 = (s32[]{:T(128)}, f32[8,64,64]{2,1,0:T(8,128)S(1)}, f32[8]{0:T(128)S(1)}, f32[8,64,64]{2,1,0:T(8,128)S(1)}, s32[]{:T(128)}, /*index=5*/s32[]{:T(128)}) while((s32[]{:T(128)}, f32[8,64,64]{2,1,0:T(8,128)S(1)}, f32[8]{0:T(128)S(1)}, f32[8,64,64]{2,1,0:T(8,128)S(1)}, s32[]{:T(128)}, /*index=5*/s32[]{:T(128)}) %tuple.92), condition=%wide.region_17.18_spmd.clone, body=%wide.region_16.17_spmd.clone.sunk | while | flops 163843 | bytes 786583 | solution.py:110
  549.8 3.5 collective-permute-done.2
  556.8 3.5 collective-permute-done.2
  567.4 5.4 collective-permute-start.2
  575.4 6.5 collective-permute-start.2
  584.6 6.5 collective-permute-start.2
  594.3 6.8 collective-permute-start.2
  604.8 6.6 collective-permute-start.2
  614.0 6.3 collective-permute-start.2
  622.9 6.5 collective-permute-start.2
  632.1 6.5 collective-permute-start.2
  641.2 6.5 collective-permute-start.2
  650.3 6.5 collective-permute-start.2
  659.7 6.8 collective-permute-start.2
  669.1 6.8 collective-permute-start.2
  679.1 15.2 %psum.23 = f32[128]{0:T(128)S(1)} all-reduce(f32[128]{0:T(128)S(1)} %multiply_reduce_fusion), channel_id=1, replica_groups=mesh['section'=2,'seq'=16,'mp'=8] {'mp'}, use_global_device_ids=true, to_apply=%region_19.20 | all-reduce | flops 128 | bytes 1024 | tf_op jit(solution)/shard_map/psum | solution.py:120
  694.3 4.6 convolution_convert_fusion
  698.9 43.8 %reduce-scatter.8.cloned.1.call-done = bf16[128,448]{0,1:T(8,128)(2,1)} async-done(((bf16[128,3584]{0,1:T(8,128)(2,1)}), bf16[128,448]{0,1:T(8,128)(2,1)}) %reduce-scatter.8.cloned.1.call-update) | async-done | bytes 114704 | tf_op jit(solution)/shard_map/reduce_scatter | solution.py:124
  (301 shorter events, 201.7 us)
Async XLA Ops:
  6.5 42.4 %copy-start = (bf16[1,3584,128]{2,1,0:T(8,128)(2,1)S(1)}, bf16[1,3584,128]{2,1,0:T(8,128)(2,1)}, u32[]{:S(2)}) copy-start(bf16[1,3584,128]{2,1,0:T(8,128)(2,1)} %param.23) | copy-start | bytes 2752516
  8.6 34.4 %all-to-all-start = ((bf16[8,128,448]{1,2,0:T(8,128)(2,1)}), bf16[8,128,448]{1,2,0:T(8,128)(2,1)S(1)}, u32[]{:S(2)}, u32[]{:S(2)}) async-start(bf16[8,128,448]{1,2,0:T(8,128)(2,1)} %stack.12), calls=%async_computation | async-start | bytes 1835008 | tf_op jit(solution)/shard_map/all_to_all | solution.py:77
  17.0 236.2 %reduce-scatter.4.cloned.1.call-start = ((), (), s32[]{:S(2)}) async-start(), calls=%async_computation.6 | async-start | bytes 1032192 | tf_op jit(solution)/shard_map/reduce_scatter | solution.py:124
  17.2 16.6 %collective-permute-start.3 = (s32[3]{0:T(128)S(1)}, s32[3]{0:T(128)S(1)}, u32[]{:S(2)}, u32[]{:S(2)}) collective-permute-start(s32[3]{0:T(128)S(1)} %get-tuple-element.173), channel_id=1, source_target_pairs={{0,8},{8,16},{16,24},{24,32},{32,40},{40,48},{48,56},{56,64},{64,7... | collective-permute-start | bytes 44 | tf_op jit(solution)/shard_map/ppermute | solution.py:15
  20.6 15.2 %collective-permute-start.9 = (s32[3]{0:T(128)S(1)}, s32[3]{0:T(128)S(1)}, u32[]{:S(2)}, u32[]{:S(2)}) collective-permute-start(s32[3]{0:T(128)S(1)} %get-tuple-element.172), channel_id=1, source_target_pairs={{0,8},{8,16},{16,24},{24,32},{32,40},{40,48},{48,56},{56,64},{64,7... | collective-permute-start | bytes 44 | tf_op jit(solution)/shard_map/ppermute | solution.py:15
  49.4 5.5 collective-permute-start.4
  56.2 132.2 %copy-start.9 = (f32[1,8]{1,0:T(1,128)S(1)}, f32[1,8]{1,0:T(1,128)}, u32[]{:S(2)}) copy-start(f32[1,8]{1,0:T(1,128)} %param.29) | copy-start | bytes 100
  56.3 6.9 collective-permute-start
  63.3 6.9 collective-permute-start
  70.3 6.9 collective-permute-start
  77.4 7.9 %collective-permute-start = (bf16[8,64,64]{2,1,0:T(8,128)(2,1)S(1)}, bf16[8,64,64]{2,1,0:T(8,128)(2,1)S(1)}, u32[]{:S(2)}, u32[]{:S(2)}) collective-permute-start(bf16[8,64,64]{2,1,0:T(8,128)(2,1)S(1)} %fusion.131), channel_id=1, source_target_pairs={{0,8},{8,16},{16,24},{24,32},{32,40},{40,48},{48,56},{56,64},{64,7... | collective-permute-start | bytes 196616 | tf_op jit(solution)/shard_map/while/body/eval_jaxpr/ppermute | solution.py:15
  85.4 9.0 %collective-permute-start = (bf16[8,64,64]{2,1,0:T(8,128)(2,1)S(1)}, bf16[8,64,64]{2,1,0:T(8,128)(2,1)S(1)}, u32[]{:S(2)}, u32[]{:S(2)}) collective-permute-start(bf16[8,64,64]{2,1,0:T(8,128)(2,1)S(1)} %fusion.131), channel_id=1, source_target_pairs={{0,8},{8,16},{16,24},{24,32},{32,40},{40,48},{48,56},{56,64},{64,7... | collective-permute-start | bytes 196616 | tf_op jit(solution)/shard_map/while/body/eval_jaxpr/ppermute | solution.py:15
  94.5 9.6 %collective-permute-start = (bf16[8,64,64]{2,1,0:T(8,128)(2,1)S(1)}, bf16[8,64,64]{2,1,0:T(8,128)(2,1)S(1)}, u32[]{:S(2)}, u32[]{:S(2)}) collective-permute-start(bf16[8,64,64]{2,1,0:T(8,128)(2,1)S(1)} %fusion.131), channel_id=1, source_target_pairs={{0,8},{8,16},{16,24},{24,32},{32,40},{40,48},{48,56},{56,64},{64,7... | collective-permute-start | bytes 196616 | tf_op jit(solution)/shard_map/while/body/eval_jaxpr/ppermute | solution.py:15
  104.3 10.3 %collective-permute-start = (bf16[8,64,64]{2,1,0:T(8,128)(2,1)S(1)}, bf16[8,64,64]{2,1,0:T(8,128)(2,1)S(1)}, u32[]{:S(2)}, u32[]{:S(2)}) collective-permute-start(bf16[8,64,64]{2,1,0:T(8,128)(2,1)S(1)} %fusion.131), channel_id=1, source_target_pairs={{0,8},{8,16},{16,24},{24,32},{32,40},{40,48},{48,56},{56,64},{64,7... | collective-permute-start | bytes 196616 | tf_op jit(solution)/shard_map/while/body/eval_jaxpr/ppermute | solution.py:15
  114.8 9.1 %collective-permute-start = (bf16[8,64,64]{2,1,0:T(8,128)(2,1)S(1)}, bf16[8,64,64]{2,1,0:T(8,128)(2,1)S(1)}, u32[]{:S(2)}, u32[]{:S(2)}) collective-permute-start(bf16[8,64,64]{2,1,0:T(8,128)(2,1)S(1)} %fusion.131), channel_id=1, source_target_pairs={{0,8},{8,16},{16,24},{24,32},{32,40},{40,48},{48,56},{56,64},{64,7... | collective-permute-start | bytes 196616 | tf_op jit(solution)/shard_map/while/body/eval_jaxpr/ppermute | solution.py:15
  124.0 8.8 %collective-permute-start = (bf16[8,64,64]{2,1,0:T(8,128)(2,1)S(1)}, bf16[8,64,64]{2,1,0:T(8,128)(2,1)S(1)}, u32[]{:S(2)}, u32[]{:S(2)}) collective-permute-start(bf16[8,64,64]{2,1,0:T(8,128)(2,1)S(1)} %fusion.131), channel_id=1, source_target_pairs={{0,8},{8,16},{16,24},{24,32},{32,40},{40,48},{48,56},{56,64},{64,7... | collective-permute-start | bytes 196616 | tf_op jit(solution)/shard_map/while/body/eval_jaxpr/ppermute | solution.py:15
  132.9 9.0 %collective-permute-start = (bf16[8,64,64]{2,1,0:T(8,128)(2,1)S(1)}, bf16[8,64,64]{2,1,0:T(8,128)(2,1)S(1)}, u32[]{:S(2)}, u32[]{:S(2)}) collective-permute-start(bf16[8,64,64]{2,1,0:T(8,128)(2,1)S(1)} %fusion.131), channel_id=1, source_target_pairs={{0,8},{8,16},{16,24},{24,32},{32,40},{40,48},{48,56},{56,64},{64,7... | collective-permute-start | bytes 196616 | tf_op jit(solution)/shard_map/while/body/eval_jaxpr/ppermute | solution.py:15
  142.1 9.0 %collective-permute-start = (bf16[8,64,64]{2,1,0:T(8,128)(2,1)S(1)}, bf16[8,64,64]{2,1,0:T(8,128)(2,1)S(1)}, u32[]{:S(2)}, u32[]{:S(2)}) collective-permute-start(bf16[8,64,64]{2,1,0:T(8,128)(2,1)S(1)} %fusion.131), channel_id=1, source_target_pairs={{0,8},{8,16},{16,24},{24,32},{32,40},{40,48},{48,56},{56,64},{64,7... | collective-permute-start | bytes 196616 | tf_op jit(solution)/shard_map/while/body/eval_jaxpr/ppermute | solution.py:15
  151.2 9.0 %collective-permute-start = (bf16[8,64,64]{2,1,0:T(8,128)(2,1)S(1)}, bf16[8,64,64]{2,1,0:T(8,128)(2,1)S(1)}, u32[]{:S(2)}, u32[]{:S(2)}) collective-permute-start(bf16[8,64,64]{2,1,0:T(8,128)(2,1)S(1)} %fusion.131), channel_id=1, source_target_pairs={{0,8},{8,16},{16,24},{24,32},{32,40},{40,48},{48,56},{56,64},{64,7... | collective-permute-start | bytes 196616 | tf_op jit(solution)/shard_map/while/body/eval_jaxpr/ppermute | solution.py:15
  160.3 9.2 %collective-permute-start = (bf16[8,64,64]{2,1,0:T(8,128)(2,1)S(1)}, bf16[8,64,64]{2,1,0:T(8,128)(2,1)S(1)}, u32[]{:S(2)}, u32[]{:S(2)}) collective-permute-start(bf16[8,64,64]{2,1,0:T(8,128)(2,1)S(1)} %fusion.131), channel_id=1, source_target_pairs={{0,8},{8,16},{16,24},{24,32},{32,40},{40,48},{48,56},{56,64},{64,7... | collective-permute-start | bytes 196616 | tf_op jit(solution)/shard_map/while/body/eval_jaxpr/ppermute | solution.py:15
  169.7 9.3 %collective-permute-start = (bf16[8,64,64]{2,1,0:T(8,128)(2,1)S(1)}, bf16[8,64,64]{2,1,0:T(8,128)(2,1)S(1)}, u32[]{:S(2)}, u32[]{:S(2)}) collective-permute-start(bf16[8,64,64]{2,1,0:T(8,128)(2,1)S(1)} %fusion.131), channel_id=1, source_target_pairs={{0,8},{8,16},{16,24},{24,32},{32,40},{40,48},{48,56},{56,64},{64,7... | collective-permute-start | bytes 196616 | tf_op jit(solution)/shard_map/while/body/eval_jaxpr/ppermute | solution.py:15
  179.1 9.3 %collective-permute-start = (bf16[8,64,64]{2,1,0:T(8,128)(2,1)S(1)}, bf16[8,64,64]{2,1,0:T(8,128)(2,1)S(1)}, u32[]{:S(2)}, u32[]{:S(2)}) collective-permute-start(bf16[8,64,64]{2,1,0:T(8,128)(2,1)S(1)} %fusion.131), channel_id=1, source_target_pairs={{0,8},{8,16},{16,24},{24,32},{32,40},{40,48},{48,56},{56,64},{64,7... | collective-permute-start | bytes 196616 | tf_op jit(solution)/shard_map/while/body/eval_jaxpr/ppermute | solution.py:15
  204.8 48.5 %copy-start.1 = (bf16[2,128,448]{1,2,0:T(8,128)(2,1)S(1)}, bf16[2,128,448]{1,2,0:T(8,128)(2,1)}, u32[]{:S(2)}) copy-start(bf16[2,128,448]{1,2,0:T(8,128)(2,1)} %param.19) | copy-start | bytes 688132
  254.2 2.2 collective-permute-start.5
  257.6 30.8 %all-to-all-start.1 = ((bf16[8,128,448]{1,2,0:T(8,128)(2,1)}), bf16[8,128,448]{1,2,0:T(8,128)(2,1)S(1)}, u32[]{:S(2)}, u32[]{:S(2)}) async-start(bf16[8,128,448]{1,2,0:T(8,128)(2,1)} %stack.13), calls=%async_computation.2 | async-start | bytes 1835008 | tf_op jit(solution)/shard_map/all_to_all | solution.py:77
  261.9 236.1 %reduce-scatter.6.cloned.1.call-start = ((), (), s32[]{:S(2)}) async-start(), calls=%async_computation.7 | async-start | bytes 1032192 | tf_op jit(solution)/shard_map/reduce_scatter | solution.py:124
  262.1 5.5 collective-permute-start.6
  294.8 5.5 collective-permute-start.7
  301.7 6.9 collective-permute-start.1
  308.7 6.9 collective-permute-start.1
  315.7 6.9 collective-permute-start.1
  322.7 7.8 %collective-permute-start.1 = (bf16[8,64,64]{2,1,0:T(8,128)(2,1)S(1)}, bf16[8,64,64]{2,1,0:T(8,128)(2,1)S(1)}, u32[]{:S(2)}, u32[]{:S(2)}) collective-permute-start(bf16[8,64,64]{2,1,0:T(8,128)(2,1)S(1)} %fusion.132), channel_id=1, source_target_pairs={{0,8},{8,16},{16,24},{24,32},{32,40},{40,48},{48,56},{56,64},{64,7... | collective-permute-start | bytes 196616 | tf_op jit(solution)/shard_map/while/body/eval_jaxpr/ppermute | solution.py:15
  330.7 9.0 %collective-permute-start.1 = (bf16[8,64,64]{2,1,0:T(8,128)(2,1)S(1)}, bf16[8,64,64]{2,1,0:T(8,128)(2,1)S(1)}, u32[]{:S(2)}, u32[]{:S(2)}) collective-permute-start(bf16[8,64,64]{2,1,0:T(8,128)(2,1)S(1)} %fusion.132), channel_id=1, source_target_pairs={{0,8},{8,16},{16,24},{24,32},{32,40},{40,48},{48,56},{56,64},{64,7... | collective-permute-start | bytes 196616 | tf_op jit(solution)/shard_map/while/body/eval_jaxpr/ppermute | solution.py:15
  339.8 9.6 %collective-permute-start.1 = (bf16[8,64,64]{2,1,0:T(8,128)(2,1)S(1)}, bf16[8,64,64]{2,1,0:T(8,128)(2,1)S(1)}, u32[]{:S(2)}, u32[]{:S(2)}) collective-permute-start(bf16[8,64,64]{2,1,0:T(8,128)(2,1)S(1)} %fusion.132), channel_id=1, source_target_pairs={{0,8},{8,16},{16,24},{24,32},{32,40},{40,48},{48,56},{56,64},{64,7... | collective-permute-start | bytes 196616 | tf_op jit(solution)/shard_map/while/body/eval_jaxpr/ppermute | solution.py:15
  349.6 10.3 %collective-permute-start.1 = (bf16[8,64,64]{2,1,0:T(8,128)(2,1)S(1)}, bf16[8,64,64]{2,1,0:T(8,128)(2,1)S(1)}, u32[]{:S(2)}, u32[]{:S(2)}) collective-permute-start(bf16[8,64,64]{2,1,0:T(8,128)(2,1)S(1)} %fusion.132), channel_id=1, source_target_pairs={{0,8},{8,16},{16,24},{24,32},{32,40},{40,48},{48,56},{56,64},{64,7... | collective-permute-start | bytes 196616 | tf_op jit(solution)/shard_map/while/body/eval_jaxpr/ppermute | solution.py:15
  360.0 9.0 %collective-permute-start.1 = (bf16[8,64,64]{2,1,0:T(8,128)(2,1)S(1)}, bf16[8,64,64]{2,1,0:T(8,128)(2,1)S(1)}, u32[]{:S(2)}, u32[]{:S(2)}) collective-permute-start(bf16[8,64,64]{2,1,0:T(8,128)(2,1)S(1)} %fusion.132), channel_id=1, source_target_pairs={{0,8},{8,16},{16,24},{24,32},{32,40},{40,48},{48,56},{56,64},{64,7... | collective-permute-start | bytes 196616 | tf_op jit(solution)/shard_map/while/body/eval_jaxpr/ppermute | solution.py:15
  369.2 8.8 %collective-permute-start.1 = (bf16[8,64,64]{2,1,0:T(8,128)(2,1)S(1)}, bf16[8,64,64]{2,1,0:T(8,128)(2,1)S(1)}, u32[]{:S(2)}, u32[]{:S(2)}) collective-permute-start(bf16[8,64,64]{2,1,0:T(8,128)(2,1)S(1)} %fusion.132), channel_id=1, source_target_pairs={{0,8},{8,16},{16,24},{24,32},{32,40},{40,48},{48,56},{56,64},{64,7... | collective-permute-start | bytes 196616 | tf_op jit(solution)/shard_map/while/body/eval_jaxpr/ppermute | solution.py:15
  378.2 9.0 %collective-permute-start.1 = (bf16[8,64,64]{2,1,0:T(8,128)(2,1)S(1)}, bf16[8,64,64]{2,1,0:T(8,128)(2,1)S(1)}, u32[]{:S(2)}, u32[]{:S(2)}) collective-permute-start(bf16[8,64,64]{2,1,0:T(8,128)(2,1)S(1)} %fusion.132), channel_id=1, source_target_pairs={{0,8},{8,16},{16,24},{24,32},{32,40},{40,48},{48,56},{56,64},{64,7... | collective-permute-start | bytes 196616 | tf_op jit(solution)/shard_map/while/body/eval_jaxpr/ppermute | solution.py:15
  387.3 9.0 %collective-permute-start.1 = (bf16[8,64,64]{2,1,0:T(8,128)(2,1)S(1)}, bf16[8,64,64]{2,1,0:T(8,128)(2,1)S(1)}, u32[]{:S(2)}, u32[]{:S(2)}) collective-permute-start(bf16[8,64,64]{2,1,0:T(8,128)(2,1)S(1)} %fusion.132), channel_id=1, source_target_pairs={{0,8},{8,16},{16,24},{24,32},{32,40},{40,48},{48,56},{56,64},{64,7... | collective-permute-start | bytes 196616 | tf_op jit(solution)/shard_map/while/body/eval_jaxpr/ppermute | solution.py:15
  396.4 9.0 %collective-permute-start.1 = (bf16[8,64,64]{2,1,0:T(8,128)(2,1)S(1)}, bf16[8,64,64]{2,1,0:T(8,128)(2,1)S(1)}, u32[]{:S(2)}, u32[]{:S(2)}) collective-permute-start(bf16[8,64,64]{2,1,0:T(8,128)(2,1)S(1)} %fusion.132), channel_id=1, source_target_pairs={{0,8},{8,16},{16,24},{24,32},{32,40},{40,48},{48,56},{56,64},{64,7... | collective-permute-start | bytes 196616 | tf_op jit(solution)/shard_map/while/body/eval_jaxpr/ppermute | solution.py:15
  405.6 9.2 %collective-permute-start.1 = (bf16[8,64,64]{2,1,0:T(8,128)(2,1)S(1)}, bf16[8,64,64]{2,1,0:T(8,128)(2,1)S(1)}, u32[]{:S(2)}, u32[]{:S(2)}) collective-permute-start(bf16[8,64,64]{2,1,0:T(8,128)(2,1)S(1)} %fusion.132), channel_id=1, source_target_pairs={{0,8},{8,16},{16,24},{24,32},{32,40},{40,48},{48,56},{56,64},{64,7... | collective-permute-start | bytes 196616 | tf_op jit(solution)/shard_map/while/body/eval_jaxpr/ppermute | solution.py:15
  414.9 9.3 %collective-permute-start.1 = (bf16[8,64,64]{2,1,0:T(8,128)(2,1)S(1)}, bf16[8,64,64]{2,1,0:T(8,128)(2,1)S(1)}, u32[]{:S(2)}, u32[]{:S(2)}) collective-permute-start(bf16[8,64,64]{2,1,0:T(8,128)(2,1)S(1)} %fusion.132), channel_id=1, source_target_pairs={{0,8},{8,16},{16,24},{24,32},{32,40},{40,48},{48,56},{56,64},{64,7... | collective-permute-start | bytes 196616 | tf_op jit(solution)/shard_map/while/body/eval_jaxpr/ppermute | solution.py:15
  424.4 9.3 %collective-permute-start.1 = (bf16[8,64,64]{2,1,0:T(8,128)(2,1)S(1)}, bf16[8,64,64]{2,1,0:T(8,128)(2,1)S(1)}, u32[]{:S(2)}, u32[]{:S(2)}) collective-permute-start(bf16[8,64,64]{2,1,0:T(8,128)(2,1)S(1)} %fusion.132), channel_id=1, source_target_pairs={{0,8},{8,16},{16,24},{24,32},{32,40},{40,48},{48,56},{56,64},{64,7... | collective-permute-start | bytes 196616 | tf_op jit(solution)/shard_map/while/body/eval_jaxpr/ppermute | solution.py:15
  449.6 48.5 %copy-start.5 = (bf16[128,448]{0,1:T(8,128)(2,1)S(1)}, bf16[128,448]{0,1:T(8,128)(2,1)}, u32[]{:S(2)}) copy-start(bf16[128,448]{0,1:T(8,128)(2,1)} %copy-done.4) | copy-start | bytes 344068
  499.0 2.2 collective-permute-start.8
  502.3 30.8 %all-to-all-start.2 = ((bf16[8,128,448]{1,2,0:T(8,128)(2,1)}), bf16[8,128,448]{1,2,0:T(8,128)(2,1)S(1)}, u32[]{:S(2)}, u32[]{:S(2)}) async-start(bf16[8,128,448]{1,2,0:T(8,128)(2,1)} %stack.15), calls=%async_computation.4 | async-start | bytes 1835008 | tf_op jit(solution)/shard_map/all_to_all | solution.py:77
  506.6 236.1 %reduce-scatter.8.cloned.1.call-start = ((), (), s32[]{:S(2)}) async-start(), calls=%async_computation.8 | async-start | bytes 1032192 | tf_op jit(solution)/shard_map/reduce_scatter | solution.py:124
  539.5 5.5 collective-permute-start.10
  546.4 6.9 collective-permute-start.2
  553.4 6.9 collective-permute-start.2
  560.4 6.9 collective-permute-start.2
  567.4 7.9 %collective-permute-start.2 = (bf16[8,64,64]{2,1,0:T(8,128)(2,1)S(1)}, bf16[8,64,64]{2,1,0:T(8,128)(2,1)S(1)}, u32[]{:S(2)}, u32[]{:S(2)}) collective-permute-start(bf16[8,64,64]{2,1,0:T(8,128)(2,1)S(1)} %fusion.133), channel_id=1, source_target_pairs={{0,8},{8,16},{16,24},{24,32},{32,40},{40,48},{48,56},{56,64},{64,7... | collective-permute-start | bytes 196616 | tf_op jit(solution)/shard_map/while/body/eval_jaxpr/ppermute | solution.py:15
  575.4 9.0 %collective-permute-start.2 = (bf16[8,64,64]{2,1,0:T(8,128)(2,1)S(1)}, bf16[8,64,64]{2,1,0:T(8,128)(2,1)S(1)}, u32[]{:S(2)}, u32[]{:S(2)}) collective-permute-start(bf16[8,64,64]{2,1,0:T(8,128)(2,1)S(1)} %fusion.133), channel_id=1, source_target_pairs={{0,8},{8,16},{16,24},{24,32},{32,40},{40,48},{48,56},{56,64},{64,7... | collective-permute-start | bytes 196616 | tf_op jit(solution)/shard_map/while/body/eval_jaxpr/ppermute | solution.py:15
  584.6 9.6 %collective-permute-start.2 = (bf16[8,64,64]{2,1,0:T(8,128)(2,1)S(1)}, bf16[8,64,64]{2,1,0:T(8,128)(2,1)S(1)}, u32[]{:S(2)}, u32[]{:S(2)}) collective-permute-start(bf16[8,64,64]{2,1,0:T(8,128)(2,1)S(1)} %fusion.133), channel_id=1, source_target_pairs={{0,8},{8,16},{16,24},{24,32},{32,40},{40,48},{48,56},{56,64},{64,7... | collective-permute-start | bytes 196616 | tf_op jit(solution)/shard_map/while/body/eval_jaxpr/ppermute | solution.py:15
  594.3 10.3 %collective-permute-start.2 = (bf16[8,64,64]{2,1,0:T(8,128)(2,1)S(1)}, bf16[8,64,64]{2,1,0:T(8,128)(2,1)S(1)}, u32[]{:S(2)}, u32[]{:S(2)}) collective-permute-start(bf16[8,64,64]{2,1,0:T(8,128)(2,1)S(1)} %fusion.133), channel_id=1, source_target_pairs={{0,8},{8,16},{16,24},{24,32},{32,40},{40,48},{48,56},{56,64},{64,7... | collective-permute-start | bytes 196616 | tf_op jit(solution)/shard_map/while/body/eval_jaxpr/ppermute | solution.py:15
  604.8 9.1 %collective-permute-start.2 = (bf16[8,64,64]{2,1,0:T(8,128)(2,1)S(1)}, bf16[8,64,64]{2,1,0:T(8,128)(2,1)S(1)}, u32[]{:S(2)}, u32[]{:S(2)}) collective-permute-start(bf16[8,64,64]{2,1,0:T(8,128)(2,1)S(1)} %fusion.133), channel_id=1, source_target_pairs={{0,8},{8,16},{16,24},{24,32},{32,40},{40,48},{48,56},{56,64},{64,7... | collective-permute-start | bytes 196616 | tf_op jit(solution)/shard_map/while/body/eval_jaxpr/ppermute | solution.py:15
  614.0 8.8 %collective-permute-start.2 = (bf16[8,64,64]{2,1,0:T(8,128)(2,1)S(1)}, bf16[8,64,64]{2,1,0:T(8,128)(2,1)S(1)}, u32[]{:S(2)}, u32[]{:S(2)}) collective-permute-start(bf16[8,64,64]{2,1,0:T(8,128)(2,1)S(1)} %fusion.133), channel_id=1, source_target_pairs={{0,8},{8,16},{16,24},{24,32},{32,40},{40,48},{48,56},{56,64},{64,7... | collective-permute-start | bytes 196616 | tf_op jit(solution)/shard_map/while/body/eval_jaxpr/ppermute | solution.py:15
  622.9 9.0 %collective-permute-start.2 = (bf16[8,64,64]{2,1,0:T(8,128)(2,1)S(1)}, bf16[8,64,64]{2,1,0:T(8,128)(2,1)S(1)}, u32[]{:S(2)}, u32[]{:S(2)}) collective-permute-start(bf16[8,64,64]{2,1,0:T(8,128)(2,1)S(1)} %fusion.133), channel_id=1, source_target_pairs={{0,8},{8,16},{16,24},{24,32},{32,40},{40,48},{48,56},{56,64},{64,7... | collective-permute-start | bytes 196616 | tf_op jit(solution)/shard_map/while/body/eval_jaxpr/ppermute | solution.py:15
  632.1 9.0 %collective-permute-start.2 = (bf16[8,64,64]{2,1,0:T(8,128)(2,1)S(1)}, bf16[8,64,64]{2,1,0:T(8,128)(2,1)S(1)}, u32[]{:S(2)}, u32[]{:S(2)}) collective-permute-start(bf16[8,64,64]{2,1,0:T(8,128)(2,1)S(1)} %fusion.133), channel_id=1, source_target_pairs={{0,8},{8,16},{16,24},{24,32},{32,40},{40,48},{48,56},{56,64},{64,7... | collective-permute-start | bytes 196616 | tf_op jit(solution)/shard_map/while/body/eval_jaxpr/ppermute | solution.py:15
  641.2 9.0 %collective-permute-start.2 = (bf16[8,64,64]{2,1,0:T(8,128)(2,1)S(1)}, bf16[8,64,64]{2,1,0:T(8,128)(2,1)S(1)}, u32[]{:S(2)}, u32[]{:S(2)}) collective-permute-start(bf16[8,64,64]{2,1,0:T(8,128)(2,1)S(1)} %fusion.133), channel_id=1, source_target_pairs={{0,8},{8,16},{16,24},{24,32},{32,40},{40,48},{48,56},{56,64},{64,7... | collective-permute-start | bytes 196616 | tf_op jit(solution)/shard_map/while/body/eval_jaxpr/ppermute | solution.py:15
  650.3 9.2 %collective-permute-start.2 = (bf16[8,64,64]{2,1,0:T(8,128)(2,1)S(1)}, bf16[8,64,64]{2,1,0:T(8,128)(2,1)S(1)}, u32[]{:S(2)}, u32[]{:S(2)}) collective-permute-start(bf16[8,64,64]{2,1,0:T(8,128)(2,1)S(1)} %fusion.133), channel_id=1, source_target_pairs={{0,8},{8,16},{16,24},{24,32},{32,40},{40,48},{48,56},{56,64},{64,7... | collective-permute-start | bytes 196616 | tf_op jit(solution)/shard_map/while/body/eval_jaxpr/ppermute | solution.py:15
  659.7 9.3 %collective-permute-start.2 = (bf16[8,64,64]{2,1,0:T(8,128)(2,1)S(1)}, bf16[8,64,64]{2,1,0:T(8,128)(2,1)S(1)}, u32[]{:S(2)}, u32[]{:S(2)}) collective-permute-start(bf16[8,64,64]{2,1,0:T(8,128)(2,1)S(1)} %fusion.133), channel_id=1, source_target_pairs={{0,8},{8,16},{16,24},{24,32},{32,40},{40,48},{48,56},{56,64},{64,7... | collective-permute-start | bytes 196616 | tf_op jit(solution)/shard_map/while/body/eval_jaxpr/ppermute | solution.py:15
  669.1 9.3 %collective-permute-start.2 = (bf16[8,64,64]{2,1,0:T(8,128)(2,1)S(1)}, bf16[8,64,64]{2,1,0:T(8,128)(2,1)S(1)}, u32[]{:S(2)}, u32[]{:S(2)}) collective-permute-start(bf16[8,64,64]{2,1,0:T(8,128)(2,1)S(1)} %fusion.133), channel_id=1, source_target_pairs={{0,8},{8,16},{16,24},{24,32},{32,40},{40,48},{48,56},{56,64},{64,7... | collective-permute-start | bytes 196616 | tf_op jit(solution)/shard_map/while/body/eval_jaxpr/ppermute | solution.py:15
  694.3 48.5 %copy-start.3 = (bf16[128,448]{0,1:T(8,128)(2,1)S(1)}, bf16[128,448]{0,1:T(8,128)(2,1)}, u32[]{:S(2)}) copy-start(bf16[128,448]{0,1:T(8,128)(2,1)} %copy-done.2) | copy-start | bytes 344068
  (12 other events, 146.0 us)
Sparse Core Ops, SparseCore 0:
  209.6 43.6 reduce-scatter.3
  454.3 43.6 reduce-scatter.5
  699.0 43.6 reduce-scatter.7
